TPU v7x, 512 devices: a whole 4x4x16 slice. The times are simulated.
512 devices in a mesh: clu: 64 (over z, y), col: 8 (over x, core).
Axes of the slice: x: 4, y: 4, z: 16, core: 2. Of those that a mesh axis runs over, the one named last changes fastest.
Arguments:
- near_blocks: float32 [64, 16, 512, 512], P('clu', 'col'), may hold values from -0.25 to 0.25
- diag_block: float32 [64, 512, 512], P('clu', 'col'), as said below
- bases: float32 [64, 512, 512], P('clu', 'col'), as said below
- near_index: int32 [64, 16], replicated, may hold values from 0 to 63, as said below
- near_mask: int32 [64, 16], P('clu'), may hold values from 0 to 1
- parent_map: int32 [64], replicated, may hold values from 0 to 31, as said below
Outputs:
- coupling: float32 [64, 16, 256, 256], P('clu', 'col')
- parent_rows: float32 [64, 256, 512], P('clu', 'col')
- redundant_factor: float32 [64, 256, 256], P('clu', 'col')
Inputs may be any that keep to these rules, and one draw needn't show every extreme that they name: `parent_map`: every parent has exactly two children. `near_index`: the slots of cluster i name the clusters (i + d) mod 64 for d = 1 to 7, d = 32 and d = -1 to -8, each offset in exactly one slot, in an order drawn per row; live slots name distinct clusters; exactly one live slot names the cluster's sibling. `diag_block`: each block is symmetric and positive definite. `bases`: each basis change is invertible.
All inputs are finite; a program needn't handle non-finite values.
Results may differ from a plain program's by a relative error of at most 0.0003.
Values sent between devices are 32-bit elements; how exact they have to be, the bound alone decides.
No kernel may reach another device: no remote copies, remote signals or barrier semaphores. Data moves between devices by JAX's collectives and lax.ppermute only.
A program may use at most 64 MiB of HBM per device.

v0:
```python
import jax
import jax.numpy as jnp
from jax import lax
from jax.sharding import PartitionSpec as P

RANK = 256


def solve_lower(factor):
    size = factor.shape[0]
    return lax.linalg.triangular_solve(
        factor, jnp.eye(size, dtype=factor.dtype), left_side=True, lower=True
    )


def pick_rows(listed, carry, piece):
    count = piece.shape[0]
    select = (listed[:, None] == jnp.arange(count, dtype=jnp.int32)[None, :]).astype(jnp.float32)
    flat = piece.reshape(count, -1)
    return jnp.dot(select, flat, precision=lax.Precision.HIGHEST).reshape(carry.shape)


def shards(near_blocks, diag_block, bases, near_index, near_mask, parent_map):
    highest = lax.Precision.HIGHEST
    columns = lax.axis_size("col")
    column = lax.axis_index("col")
    own_index = lax.axis_index("clu")
    row_count = bases.shape[1]
    leaf_size = bases.shape[2]
    redundant = leaf_size - RANK
    per_device = near_blocks.shape[1]
    slot_total = near_index.shape[1]
    listed = lax.dynamic_slice_in_dim(near_index, own_index, 1, 0)[0]
    full_diag, full_basis = (
        lax.all_gather(diag_block, "col", axis=1, tiled=True),
        lax.all_gather(bases, "col", axis=1, tiled=True),
    )
    basis = full_basis[0]
    reduced = jnp.dot(basis.T, jnp.dot(full_diag[0], basis, precision=highest), precision=highest)
    factor = jnp.linalg.cholesky(reduced[:redundant, :redundant])
    inverse = solve_lower(factor)
    couple = jnp.dot(inverse, reduced[:redundant, redundant:], precision=highest)
    schur = reduced[redundant:, redundant:] - jnp.dot(couple.T, couple, precision=highest)
    skeleton_rows = bases[:, :, redundant:]
    empty = jnp.zeros((slot_total, row_count, RANK), jnp.float32)
    picked = pick_rows(listed, empty, lax.all_gather(skeleton_rows, "clu", axis=0, tiled=True))
    grouped = picked.reshape(columns, per_device, row_count, RANK)
    routed = lax.all_to_all(grouped, "col", split_axis=0, concat_axis=2, tiled=True)
    partners = routed[0]
    middle = jnp.einsum("kab,kbr->kar", near_blocks[0], partners, precision=highest)
    coupled = jnp.einsum("ba,kbr->kar", basis, middle, precision=highest)
    solved = jnp.einsum("xy,kyr->kxr", inverse, coupled[:, :redundant], precision=highest)
    local_list = lax.dynamic_slice_in_dim(listed, column * per_device, per_device, 0)
    local_live = lax.dynamic_slice_in_dim(near_mask[0], column * per_device, per_device, 0).astype(
        jnp.float32
    )
    coupling = (
        coupled[:, redundant:] - jnp.einsum("xs,kxr->ksr", couple, solved, precision=highest)
    ) * local_live[:, None, None]
    cluster_ids = jnp.arange(parent_map.shape[0], dtype=jnp.int32)
    own_parent = lax.dynamic_slice_in_dim(parent_map, own_index, 1, 0)[0]
    same = (parent_map == own_parent) & (cluster_ids != own_index)
    sibling = jnp.sum(jnp.where(same, cluster_ids, 0))
    matches = local_live * (local_list == sibling).astype(jnp.float32)
    side = jnp.einsum("k,kab->ab", matches, coupling, precision=highest)
    first = (own_index < sibling).astype(jnp.float32)
    side_wide = jnp.concatenate([(1.0 - first) * side, first * side], axis=1)
    summed = lax.psum_scatter(side_wide, "col", scatter_dimension=0, tiled=True)
    merged_count = summed.shape[0]
    schur_rows = lax.dynamic_slice_in_dim(schur, column * merged_count, merged_count, 0)
    parent_rows = summed + jnp.concatenate([first * schur_rows, (1.0 - first) * schur_rows], axis=1)
    factor_count = redundant // columns
    factor_rows = lax.dynamic_slice_in_dim(factor, column * factor_count, factor_count, 0)
    return (coupling[None], parent_rows[None], factor_rows[None])


def solution(mesh):
    in_specs = (
        P("clu", "col", None, None),
        P("clu", "col", None),
        P("clu", "col", None),
        P(),
        P("clu", None),
        P(),
    )
    out_specs = (P("clu", "col", None, None), P("clu", "col", None), P("clu", "col", None))
    return jax.shard_map(shards, mesh=mesh, in_specs=in_specs, out_specs=out_specs, check_vma=False)
```

profile of v0, /device:TPU:8, one launch (start us, length us, event | category | flops | bytes accessed | tf_op | source)
XLA Modules:
  0.0 305.6 jit_solution(5359909306304034356)
XLA Ops:
  8.7 1.5 slice.61
  12.5 1.9 fusion.34
  15.1 1.5 compare_reduce_fusion
  18.6 26.8 %all-gather.6.cloned.1.call-done = f32[1,512,512]{2,1,0:T(8,128)} async-done(((f32[1,64,512]{2,1,0:T(8,128)}), f32[1,512,512]{2,1,0:T(8,128)}) %all-gather.6.cloned.1.call-update) | async-done | bytes 1048592 | tf_op jit(solution)/shard_map/all_gather | solution.py:36
  45.4 33.0 %all-gather.8.cloned.1.call-done = f32[1,512,512]{2,1,0:T(8,128)} async-done(((f32[1,64,512]{2,1,0:T(8,128)}), f32[1,512,512]{2,1,0:T(8,128)}) %all-gather.8.cloned.1.call-update) | async-done | bytes 1048592 | tf_op jit(solution)/shard_map/all_gather | solution.py:35
  78.5 3.4 %fusion.9 = f32[512,512]{1,0:T(8,128)S(1)} fusion(f32[1,512,512]{2,1,0:T(8,128)} %all-gather.8.cloned.1.call-done, f32[1,512,512]{2,1,0:T(8,128)} %all-gather.6.cloned.1.call-done), kind=kOutput, calls=%fused_computation.16 | convolution fusion | flops 1610612736 | bytes 3145728 | tf_op jit(solution)/shard_map/dot_general | solution.py:39
  81.9 3.1 %convolution_bitcast_fusion = f32[512,512]{0,1:T(8,128)S(1)} fusion(f32[512,512]{1,0:T(8,128)S(1)} %fusion.9, f32[1,512,512]{2,1,0:T(8,128)} %all-gather.6.cloned.1.call-done), kind=kOutput, calls=%fused_computation.8 | convolution fusion | flops 1610612736 | bytes 3145728 | tf_op jit(solution)/shard_map/dot_general | solution.py:39
  87.7 11.7 %cholesky.50 = f32[128,128]{1,0:T(8,128)S(1)} custom-call(f32[128,128]{1,0:T(8,128)S(1)} %cholesky.118), custom_call_target="Cholesky" | custom-call | tf_op jit(solution)/shard_map/jit(cholesky)/cholesky | solution.py:40
  99.5 9.8 %custom-call.14 = f32[1,128,128]{1,2,0:T(8,128)S(1)} custom-call(f32[1,128,128]{2,1,0:T(8,128)S(1)} %get-tuple-element.46), custom_call_target="InvertDiagBlocksLowerTriangular" | custom-call | tf_op jit(solution)/shard_map/jit(cholesky)/cholesky | solution.py:40
  111.5 11.9 %cholesky.105 = f32[128,128]{1,0:T(8,128)S(1)} custom-call(f32[128,128]{1,0:T(8,128)S(1)} %convolution_subtract_fusion.1), custom_call_target="Cholesky" | custom-call | tf_op jit(solution)/shard_map/jit(cholesky)/cholesky | solution.py:40
  125.3 1.7 fusion.21
  127.8 5.3 %while.1 = (s32[]{:T(128)}, f32[256,256]{1,0:T(8,128)S(1)}, s32[2,2]{1,0:T(2,128)S(1)}, f32[2,128,128]{2,1,0:T(8,128)}, s32[]{:T(128)}) while((s32[]{:T(128)}, f32[256,256]{1,0:T(8,128)S(1)}, s32[2,2]{1,0:T(2,128)S(1)}, f32[2,128,128]{2,1,0:T(8,128)}, s32[]{:T(128)}) %tuple.37), condition=%wide.while_cond, body=%wide.while_body.sunk | while | flops 2 | bytes 132205 | solution.py:11
  128.4 2.0 bitcast_dynamic-update-slice_fusion.2
  131.0 2.0 bitcast_dynamic-update-slice_fusion.2
  133.0 21.1 %custom-call.15 = f32[2,128,128]{1,2,0:T(8,128)} custom-call(f32[2,128,128]{2,1,0:T(8,128)} %get-tuple-element.10), custom_call_target="InvertDiagBlocksLowerTriangular" | custom-call | tf_op jit(solution)/shard_map/triangular_solve | solution.py:11
  154.1 72.9 %all-gather.4.cloned.1.call-done = f32[64,64,256]{2,1,0:T(8,128)} async-done(((f32[1,64,256]{2,1,0:T(8,128)}), f32[64,64,256]{2,1,0:T(8,128)}) %all-gather.4.cloned.1.call-update) | async-done | bytes 4194320 | tf_op jit(solution)/shard_map/all_gather | solution.py:46
  227.1 5.8 %fusion = f32[8,2,64,256]{3,0,2,1:T(8,128)S(1)} fusion(s32[8,2]{0,1:T(2,128)S(1)} %copy.36, f32[8,8,64,256]{3,2,1,0:T(8,128)} %bitcast.110), kind=kOutput, calls=%fused_computation.3 | convolution fusion | flops 201327616 | bytes 5242944 | tf_op jit(solution)/shard_map/dot_general | solution.py:20
  232.9 1.4 copy.38
  234.3 4.3 %all-to-all-start = ((f32[8,2,64,256]{3,2,1,0:T(8,128)}), f32[8,2,64,256]{3,2,1,0:T(8,128)}, u32[]{:S(2)}, u32[]{:S(2)}) async-start(f32[8,2,64,256]{3,2,1,0:T(8,128)} %copy.38), calls=%async_computation | async-start | bytes 2097152 | tf_op jit(solution)/shard_map/all_to_all | solution.py:48
  244.1 10.4 %all-to-all-done = f32[8,2,64,256]{3,2,1,0:T(8,128)} async-done(((f32[8,2,64,256]{3,2,1,0:T(8,128)}), f32[8,2,64,256]{3,2,1,0:T(8,128)}, u32[]{:S(2)}, u32[]{:S(2)}) %all-to-all-start) | async-done | bytes 1048608 | tf_op jit(solution)/shard_map/all_to_all | solution.py:48
  255.9 3.6 %fusion.4 = f32[2,512,256]{1,2,0:T(8,128)S(1)} fusion(f32[2,512,256]{2,1,0:T(8,128)S(1)} %bitcast.111, f32[1,2,512,512]{3,2,1,0:T(8,128)S(1)} %copy-done), kind=kOutput, calls=%fused_computation.7 | convolution fusion | flops 1610612736 | bytes 4194304 | tf_op jit(solution)/shard_map/kab,kbr->kar/dot_general | solution.py:50
  259.5 1.9 convolution_bitcast_fusion.1
  263.7 1.4 dynamic-slice_bitcast_fusion
  267.8 29.6 %reduce-scatter.4.cloned.1.call-done = f32[32,512]{1,0:T(8,128)} async-done(((f32[256,512]{1,0:T(8,128)}), f32[32,512]{1,0:T(8,128)}) %reduce-scatter.4.cloned.1.call-update) | async-done | bytes 65552
  (61 shorter events, 26.9 us)
Async XLA Ops:
  7.2 248.7 %copy-start = (f32[1,2,512,512]{3,2,1,0:T(8,128)S(1)}, f32[1,2,512,512]{3,2,1,0:T(8,128)}, u32[]{:S(2)}) copy-start(f32[1,2,512,512]{3,2,1,0:T(8,128)} %param.6) | copy-start | bytes 6291460
  7.2 38.3 %all-gather.6.cloned.1.call-start = ((), (), s32[]{:S(2)}) async-start(), calls=%async_computation.3 | async-start | bytes 1179648 | tf_op jit(solution)/shard_map/all_gather | solution.py:36
  7.9 70.6 %all-gather.8.cloned.1.call-start = ((), (), s32[]{:S(2)}) async-start(), calls=%async_computation.4 | async-start | bytes 1179648 | tf_op jit(solution)/shard_map/all_gather | solution.py:35
  8.7 218.4 %all-gather.4.cloned.1.call-start = ((), (), s32[]{:S(2)}) async-start(), calls=%async_computation.2 | async-start | bytes 4259840 | tf_op jit(solution)/shard_map/all_gather | solution.py:46
  84.9 148.0 %copy-start.2 = (f32[512,512]{0,1:T(8,128)}, f32[512,512]{0,1:T(8,128)S(1)}, u32[]{:S(2)}) copy-start(f32[512,512]{0,1:T(8,128)S(1)} %convolution_bitcast_fusion) | copy-start | bytes 3145732
  87.0 0.7 copy-start.6
  123.4 2.0 copy-start.5
  234.3 20.3 %all-to-all-start = ((f32[8,2,64,256]{3,2,1,0:T(8,128)}), f32[8,2,64,256]{3,2,1,0:T(8,128)}, u32[]{:S(2)}, u32[]{:S(2)}) async-start(f32[8,2,64,256]{3,2,1,0:T(8,128)} %copy.38), calls=%async_computation | async-start | bytes 2097152 | tf_op jit(solution)/shard_map/all_to_all | solution.py:48
  238.5 21.0 %copy-start.1 = (f32[1,512,512]{2,1,0:T(8,128)S(1)}, f32[1,512,512]{2,1,0:T(8,128)}, u32[]{:S(2)}) copy-start(f32[1,512,512]{2,1,0:T(8,128)} %all-gather.6.cloned.1.call-done) | copy-start | bytes 3145732
  238.5 58.8 %reduce-scatter.4.cloned.1.call-start = ((), (), s32[]{:S(2)}) async-start(), calls=%async_computation.5 | async-start | bytes 589824
  242.1 0.7 copy-start.3
  255.9 5.5 %copy-start.4 = (f32[128,256]{1,0:T(8,128)S(1)}, f32[128,256]{1,0:T(8,128)}, u32[]{:S(2)}) copy-start(f32[128,256]{1,0:T(8,128)} %copy-done.3) | copy-start | bytes 393220
Sparse Core Ops, SparseCore 0:
  10.1 35.2 all-gather.5
  47.6 30.8 all-gather.7
  82.0 145.0 all-gather.3
  263.8 33.4 reduce-scatter.3
where the time goes:
time: 307 us; the launch traced here: 306 us
  waiting for transfers between devices  174 us (57%)
  other arithmetic  63.5 us (21%)
  matrix products  26.3 us (9%)
  local copies, waits for them, and re-layouts  20.9 us (7%)
  between operations  16 us (5%)
  starting transfers between devices  4.63 us (2%)
    all_gather x1, waiting for transfers between devices, shards(): lax.all_gather(skeleton_rows, 'clu', axis=0, tiled=True)  72.9 us
    another operation x6, other arithmetic, shards(): factor = jnp.linalg.cholesky(reduced[:redundant, :redundant])  34.1 us
    all_gather x1, waiting for transfers between devices, shards(): lax.all_gather(diag_block, 'col', axis=1, tiled=True)  33 us
    unnamed x5, waiting for transfers between devices  31 us
    all_gather x1, waiting for transfers between devices, shards(): lax.all_gather(bases, 'col', axis=1, tiled=True)  26.8 us
    another operation x3, other arithmetic, solve_lower(): lax.linalg.triangular_solve(factor, jnp.eye(size, dtype=factor.dtype), le...  23.4 us
    all_to_all x1, waiting for transfers between devices, shards(): lax.all_to_all(grouped, 'col', split_axis=0, concat_axis=2, tiled=True)  10.4 us
  transfers between devices with their start and end apart: 5, of which 5 were waited for; matrix products, arithmetic and copies ran while one was open for 30% of the time, Pallas kernels for 0%

commit v1 on v0

--- a/solution.py
+++ b/solution.py
@@ -4,6 +4,13 @@
 from jax.sharding import PartitionSpec as P
 
 RANK = 256
+
+
+def exchange_gather(x, axis, along):
+    count = lax.axis_size(axis)
+    blocks = jnp.stack([x for _ in range(count)])
+    blocks = lax.all_to_all(blocks, axis, split_axis=0, concat_axis=0)
+    return jnp.concatenate(blocks, axis=along)
 
 
 def solve_lower(factor):
@@ -33,7 +40,7 @@
     listed = lax.dynamic_slice_in_dim(near_index, own_index, 1, 0)[0]
     full_diag, full_basis = (
         lax.all_gather(diag_block, "col", axis=1, tiled=True),
-        lax.all_gather(bases, "col", axis=1, tiled=True),
+        exchange_gather(bases, "col", 1),
     )
     basis = full_basis[0]
     reduced = jnp.dot(basis.T, jnp.dot(full_diag[0], basis, precision=highest), precision=highest)

time: 307 us -> 273 us (0.89)
  waiting for transfers between devices: 174 us -> 135 us
  starting transfers between devices: 4.63 us -> 8.89 us
    all_gather x1 -> x0, waiting for transfers between devices: 26.8 us -> none  [shards(): lax.all_gather(bases, 'col', axis=1, tiled=True)]
    all_gather x1, waiting for transfers between devices: 33 us -> 13.7 us  [shards(): lax.all_gather(diag_block, 'col', axis=1, tiled=True)]
    all_to_all x0 -> x1, waiting for transfers between devices: none -> 7.6 us  [exchange_gather(): blocks = lax.all_to_all(blocks, axis, split_axis=0, concat_axis=0)]
    all_to_all x0 -> x1, starting transfers between devices: none -> 4.3 us  [exchange_gather(): blocks = lax.all_to_all(blocks, axis, split_axis=0, concat_axis=0)]
    another operation x6 -> x7, local copies, waits for them, and re-layouts: 5.27 us -> 7.09 us
    unnamed x5 -> x4, waiting for transfers between devices: 31 us -> 30.2 us
  transfers between devices with their start and end apart: 5 -> 5, of which waited for: 5 -> 5; matrix products, arithmetic and copies ran while one was open for 30% -> 34% of each run, Pallas kernels for 0% -> 0%
where the time goes in v1:
time: 273 us; the launch traced here: 272 us
  waiting for transfers between devices  135 us (49%)
  other arithmetic  64.4 us (24%)
  matrix products  24.8 us (9%)
  local copies, waits for them, and re-layouts  23.5 us (9%)
  between operations  15.9 us (6%)
  starting transfers between devices  8.89 us (3%)
    all_gather x1, waiting for transfers between devices, shards(): lax.all_gather(skeleton_rows, 'clu', axis=0, tiled=True)  72.8 us
    another operation x6, other arithmetic, shards(): factor = jnp.linalg.cholesky(reduced[:redundant, :redundant])  34.1 us
    unnamed x4, waiting for transfers between devices  30.2 us
    another operation x3, other arithmetic, solve_lower(): lax.linalg.triangular_solve(factor, jnp.eye(size, dtype=factor.dtype), le...  23.3 us
    all_gather x1, waiting for transfers between devices, shards(): lax.all_gather(diag_block, 'col', axis=1, tiled=True)  13.7 us
    all_to_all x1, waiting for transfers between devices, shards(): lax.all_to_all(grouped, 'col', split_axis=0, concat_axis=2, tiled=True)  10.5 us
    all_to_all x1, waiting for transfers between devices, exchange_gather(): blocks = lax.all_to_all(blocks, axis, split_axis=0, concat_axis=0)  7.6 us
    unnamed x16, local copies, waits for them, and re-layouts  6.01 us
  transfers between devices with their start and end apart: 5, of which 5 were waited for; matrix products, arithmetic and copies ran while one was open for 34% of the time, Pallas kernels for 0%

profile of v1, /device:TPU:8, one launch (start us, length us, event | category | flops | bytes accessed | tf_op | source)
XLA Modules:
  0.0 272.3 jit_solution(15328348103734469699)
XLA Ops:
  8.0 1.5 slice.61
  9.5 2.0 stack.2
  11.5 4.3 %all-to-all-start.1 = ((f32[8,1,64,512]{3,2,1,0:T(8,128)}), f32[8,1,64,512]{3,2,1,0:T(8,128)S(1)}, u32[]{:S(2)}, u32[]{:S(2)}) async-start(f32[8,1,64,512]{3,2,1,0:T(8,128)} %stack.2), calls=%async_computation.1 | async-start | bytes 2097152 | tf_op jit(solution)/shard_map/all_to_all | solution.py:12
  18.1 1.9 fusion.31
  20.7 1.5 compare_reduce_fusion
  24.1 7.6 %all-to-all-done.1 = f32[8,1,64,512]{3,2,1,0:T(8,128)S(1)} async-done(((f32[8,1,64,512]{3,2,1,0:T(8,128)}), f32[8,1,64,512]{3,2,1,0:T(8,128)S(1)}, u32[]{:S(2)}, u32[]{:S(2)}) %all-to-all-start.1) | async-done | bytes 1048608 | tf_op jit(solution)/shard_map/all_to_all | solution.py:12
  31.7 13.7 %all-gather.5.cloned.1.call-done = f32[1,512,512]{2,1,0:T(8,128)} async-done(((f32[1,64,512]{2,1,0:T(8,128)}), f32[1,512,512]{2,1,0:T(8,128)}) %all-gather.5.cloned.1.call-update) | async-done | bytes 1048592 | tf_op jit(solution)/shard_map/all_gather | solution.py:42
  45.4 3.1 %fusion.9 = f32[512,512]{1,0:T(8,128)S(1)} fusion(f32[512,512]{1,0:T(8,128)S(1)} %bitcast.109, f32[1,512,512]{2,1,0:T(8,128)} %all-gather.5.cloned.1.call-done), kind=kOutput, calls=%fused_computation.16 | convolution fusion | flops 1610612736 | bytes 3145728 | tf_op jit(solution)/shard_map/dot_general | solution.py:46
  48.5 1.8 convolution_bitcast_fusion
  54.9 11.7 %cholesky.50 = f32[128,128]{1,0:T(8,128)S(1)} custom-call(f32[128,128]{1,0:T(8,128)S(1)} %cholesky.118), custom_call_target="Cholesky" | custom-call | tf_op jit(solution)/shard_map/jit(cholesky)/cholesky | solution.py:47
  66.7 9.8 %custom-call.14 = f32[1,128,128]{1,2,0:T(8,128)S(1)} custom-call(f32[1,128,128]{2,1,0:T(8,128)S(1)} %get-tuple-element.46), custom_call_target="InvertDiagBlocksLowerTriangular" | custom-call | tf_op jit(solution)/shard_map/jit(cholesky)/cholesky | solution.py:47
  78.7 11.9 %cholesky.105 = f32[128,128]{1,0:T(8,128)S(1)} custom-call(f32[128,128]{1,0:T(8,128)S(1)} %convolution_subtract_fusion.1), custom_call_target="Cholesky" | custom-call | tf_op jit(solution)/shard_map/jit(cholesky)/cholesky | solution.py:47
  92.5 1.7 fusion.18
  94.9 5.0 %while.1 = (s32[]{:T(128)}, f32[256,256]{1,0:T(8,128)S(1)}, s32[2,2]{1,0:T(2,128)S(1)}, f32[2,128,128]{2,1,0:T(8,128)}, s32[]{:T(128)}) while((s32[]{:T(128)}, f32[256,256]{1,0:T(8,128)S(1)}, s32[2,2]{1,0:T(2,128)S(1)}, f32[2,128,128]{2,1,0:T(8,128)}, s32[]{:T(128)}) %tuple.37), condition=%wide.while_cond, body=%wide.while_body.sunk | while | flops 2 | bytes 132205 | solution.py:18
  95.5 1.9 bitcast_dynamic-update-slice_fusion.2
  98.0 1.9 bitcast_dynamic-update-slice_fusion.2
  99.9 21.1 %custom-call.15 = f32[2,128,128]{1,2,0:T(8,128)} custom-call(f32[2,128,128]{2,1,0:T(8,128)} %get-tuple-element.10), custom_call_target="InvertDiagBlocksLowerTriangular" | custom-call | tf_op jit(solution)/shard_map/triangular_solve | solution.py:18
  121.0 72.8 %all-gather.3.cloned.1.call-done = f32[64,64,256]{2,1,0:T(8,128)} async-done(((f32[1,64,256]{2,1,0:T(8,128)}), f32[64,64,256]{2,1,0:T(8,128)}) %all-gather.3.cloned.1.call-update) | async-done | bytes 4194320 | tf_op jit(solution)/shard_map/all_gather | solution.py:53
  193.8 5.8 %fusion = f32[8,2,64,256]{3,0,2,1:T(8,128)S(1)} fusion(s32[8,2]{0,1:T(2,128)S(1)} %copy.36, f32[8,8,64,256]{3,2,1,0:T(8,128)} %bitcast.112), kind=kOutput, calls=%fused_computation.3 | convolution fusion | flops 201327616 | bytes 5242944 | tf_op jit(solution)/shard_map/dot_general | solution.py:27
  201.0 4.3 %all-to-all-start = ((f32[8,2,64,256]{3,2,1,0:T(8,128)}), f32[8,2,64,256]{3,2,1,0:T(8,128)}, u32[]{:S(2)}, u32[]{:S(2)}) async-start(f32[8,2,64,256]{3,2,1,0:T(8,128)} %copy.38), calls=%async_computation | async-start | bytes 2097152 | tf_op jit(solution)/shard_map/all_to_all | solution.py:55
  210.8 10.5 %all-to-all-done = f32[8,2,64,256]{3,2,1,0:T(8,128)} async-done(((f32[8,2,64,256]{3,2,1,0:T(8,128)}), f32[8,2,64,256]{3,2,1,0:T(8,128)}, u32[]{:S(2)}, u32[]{:S(2)}) %all-to-all-start) | async-done | bytes 1048608 | tf_op jit(solution)/shard_map/all_to_all | solution.py:55
  222.6 3.6 %fusion.4 = f32[2,512,256]{1,2,0:T(8,128)S(1)} fusion(f32[2,512,256]{2,1,0:T(8,128)S(1)} %bitcast.113, f32[1,2,512,512]{3,2,1,0:T(8,128)S(1)} %copy-done), kind=kOutput, calls=%fused_computation.7 | convolution fusion | flops 1610612736 | bytes 4194304 | tf_op jit(solution)/shard_map/kab,kbr->kar/dot_general | solution.py:57
  226.2 1.9 convolution_bitcast_fusion.1
  234.5 29.5 %reduce-scatter.4.cloned.1.call-done = f32[32,512]{1,0:T(8,128)} async-done(((f32[256,512]{1,0:T(8,128)}), f32[32,512]{1,0:T(8,128)}) %reduce-scatter.4.cloned.1.call-update) | async-done | bytes 65552
  (59 shorter events, 30.5 us)
Async XLA Ops:
  7.2 215.4 %copy-start = (f32[1,2,512,512]{3,2,1,0:T(8,128)S(1)}, f32[1,2,512,512]{3,2,1,0:T(8,128)}, u32[]{:S(2)}) copy-start(f32[1,2,512,512]{3,2,1,0:T(8,128)} %param.6) | copy-start | bytes 6291460
  7.2 38.3 %all-gather.5.cloned.1.call-start = ((), (), s32[]{:S(2)}) async-start(), calls=%async_computation.4 | async-start | bytes 1179648 | tf_op jit(solution)/shard_map/all_gather | solution.py:42
  7.9 185.9 %all-gather.3.cloned.1.call-start = ((), (), s32[]{:S(2)}) async-start(), calls=%async_computation.3 | async-start | bytes 4259840 | tf_op jit(solution)/shard_map/all_gather | solution.py:53
  11.5 20.2 %all-to-all-start.1 = ((f32[8,1,64,512]{3,2,1,0:T(8,128)}), f32[8,1,64,512]{3,2,1,0:T(8,128)S(1)}, u32[]{:S(2)}, u32[]{:S(2)}) async-start(f32[8,1,64,512]{3,2,1,0:T(8,128)} %stack.2), calls=%async_computation.1 | async-start | bytes 2097152 | tf_op jit(solution)/shard_map/all_to_all | solution.py:12
  50.4 1.0 copy-start.1
  54.2 0.7 copy-start.5
  90.6 1.9 copy-start.4
  201.0 20.3 %all-to-all-start = ((f32[8,2,64,256]{3,2,1,0:T(8,128)}), f32[8,2,64,256]{3,2,1,0:T(8,128)}, u32[]{:S(2)}, u32[]{:S(2)}) async-start(f32[8,2,64,256]{3,2,1,0:T(8,128)} %copy.38), calls=%async_computation | async-start | bytes 2097152 | tf_op jit(solution)/shard_map/all_to_all | solution.py:55
  205.2 58.7 %reduce-scatter.4.cloned.1.call-start = ((), (), s32[]{:S(2)}) async-start(), calls=%async_computation.5 | async-start | bytes 589824
  208.8 0.7 copy-start.2
  222.6 5.5 %copy-start.3 = (f32[128,256]{1,0:T(8,128)S(1)}, f32[128,256]{1,0:T(8,128)}, u32[]{:S(2)}) copy-start(f32[128,256]{1,0:T(8,128)} %copy-done.2) | copy-start | bytes 393220
Sparse Core Ops, SparseCore 0:
  10.1 35.2 all-gather.4
  49.0 144.8 all-gather.2
  230.6 33.3 reduce-scatter.3
